TPU v7x, 512 devices: a whole 4x4x16 slice. The times are simulated.
512 devices in a mesh: row: 32 (over z, y_lo), col: 16 (over y_hi, x, core).
Axes of the slice: x: 4, y: 4 (y_hi: 2, y_lo: 2; y = y_hi * 2 + y_lo), z: 16, core: 2. Of those that a mesh axis runs over, the one named last changes fastest.
Arguments:
- atom_feats: bfloat16 [32768, 128], P(('row', 'col')), may hold values from -6 to 6
- key_starts: int32 [1024], P(('row', 'col')), may hold values from -64 to 32704, as said below
- atom_counts: int32 [2048], replicated, may hold values from 8 to 24, as said below
- atom_gain: float32 [128], replicated, may hold values from 0.1 to 1.9
- w_query: bfloat16 [128, 128], replicated, may hold values from -0.5 to 0.5
- w_key: bfloat16 [128, 128], replicated, may hold values from -0.5 to 0.5
- w_value: bfloat16 [128, 128], replicated, may hold values from -0.5 to 0.5
- w_out: bfloat16 [128, 128], replicated, may hold values from -0.5 to 0.5
- w_pool: bfloat16 [128, 384], replicated, may hold values from -0.5 to 0.5
- w_back: bfloat16 [384, 128], replicated, may hold values from -0.3125 to 0.3125
- pair_state: bfloat16 [2048, 2048, 128], P('row', 'col'), may hold values from -6 to 6
- w_left: bfloat16 [384, 32], replicated, may hold values from -0.3125 to 0.3125
- w_right: bfloat16 [384, 32], replicated, may hold values from -0.3125 to 0.3125
- w_outer: bfloat16 [32, 32, 128], replicated, may hold values from -0.1875 to 0.1875
- pair_gain: float32 [128], replicated, may hold values from 0.1 to 1.9
- w_gate: bfloat16 [128, 512], replicated, may hold values from -0.5 to 0.5
- w_lift: bfloat16 [128, 512], replicated, may hold values from -0.5 to 0.5
- w_drop: bfloat16 [512, 128], replicated, may hold values from -0.25 to 0.25
Outputs:
- atom_out: bfloat16 [32768, 128], P(('row', 'col'))
- token_single: bfloat16 [2048, 384], P(('row', 'col'))
- pair_out: bfloat16 [2048, 2048, 128], P('row', 'col')
Inputs may be any that keep to these rules, and one draw needn't show every extreme that they name: key_starts[b] = 32 * b - 64 + offset, with offset a whole number from 0 to 32; the offset is 0 for the first block and 32 for the last. `atom_counts`: the counts sum to 32768.
All inputs are finite; a program needn't handle non-finite values.
Results may differ from a plain program's by a relative error of at most 0.007.
Values may be sent and summed in bfloat16 or wider, within the bound.
A program may use at most 64 MiB of HBM per device.

v0:
```python
import math
import jax
import jax.numpy as jnp
from jax import lax
from jax.sharding import PartitionSpec as P

HEADS = 4
QB = 32
KW = 128
FEWEST = 8
MOST = 24
EPSILON = 1e-05
BOTH = ("row", "col")


def shifted(block, distance):
    count = lax.axis_size(BOTH)
    route = [(i - distance, i) for i in range(count) if 0 <= i - distance < count]
    return lax.ppermute(block, BOTH, route)


def layer_norm(values, gain):
    mean_value = jnp.mean(values, axis=-1, keepdims=True)
    centred = values - mean_value
    variance = jnp.mean(centred * centred, axis=-1, keepdims=True)
    return centred * lax.rsqrt(variance + EPSILON) * gain


def project(source, weight):
    return jnp.dot(source, weight, preferred_element_type=jnp.float32).astype(jnp.bfloat16)


def atom_part(
    ext,
    feats_q,
    starts,
    first_atom,
    total_atoms,
    spans,
    atom_gain,
    w_query,
    w_key,
    w_value,
    w_out,
    w_pool,
    w_back,
):
    width = ext.shape[1]
    head = width // HEADS
    normed = layer_norm(ext.astype(jnp.float32), atom_gain).astype(jnp.bfloat16)
    keys = project(normed, w_key)
    values = project(normed, w_value)
    queries = project(normed[64:192], w_query)
    key_atom = first_atom - 96 + lax.broadcasted_iota(jnp.int32, (128, 256), 1)
    mask = (
        (key_atom >= starts) & (key_atom < starts + KW) & (key_atom >= 0) & (key_atom < total_atoms)
    )
    query_atom = first_atom - 32 + lax.broadcasted_iota(jnp.int32, (128, 1), 0)
    real = (query_atom >= 0) & (query_atom < total_atoms)
    pieces = []
    for h in range(HEADS):
        cut = slice(h * head, (h + 1) * head)
        scores = lax.dot_general(
            queries[:, cut],
            keys[:, cut],
            (((1,), (1,)), ((), ())),
            preferred_element_type=jnp.float32,
        ) * head ** (-0.5)
        raised = jnp.where(mask, jnp.exp(scores), 0.0)
        total = jnp.where(real, jnp.sum(raised, axis=-1, keepdims=True), 1.0)
        weights = (raised / total).astype(jnp.bfloat16)
        pieces.append(jnp.dot(weights, values[:, cut], preferred_element_type=jnp.float32))
    attended = jnp.concatenate(pieces, axis=1).astype(jnp.bfloat16)
    updated = (
        feats_q.astype(jnp.float32) + jnp.dot(attended, w_out, preferred_element_type=jnp.float32)
    ).astype(jnp.bfloat16)
    feature = jax.nn.relu(jnp.dot(updated, w_pool, preferred_element_type=jnp.float32)).astype(
        jnp.bfloat16
    )
    low, high = spans
    atoms = first_atom - 32 + lax.broadcasted_iota(jnp.int32, (low.shape[0], 128), 1)
    member = ((atoms >= low) & (atoms < high)).astype(jnp.bfloat16)
    pooled = jnp.dot(member, feature, preferred_element_type=jnp.float32)
    counts = jnp.maximum(high - low, 1).astype(jnp.float32)
    single = (pooled / counts).astype(jnp.bfloat16)
    back = project(single, w_back)
    lifted = lax.dot_general(
        member[:, 32:96], back, (((0,), (0,)), ((), ())), preferred_element_type=jnp.float32
    )
    atom_out = (updated[32:96].astype(jnp.float32) + lifted).astype(jnp.bfloat16)
    return (atom_out, single)


def per_device(
    atom_feats,
    key_starts,
    atom_counts,
    atom_gain,
    w_query,
    w_key,
    w_value,
    w_out,
    w_pool,
    w_back,
    pair_state,
    w_left,
    w_right,
    w_outer,
    pair_gain,
    w_gate,
    w_lift,
    w_drop,
):
    atom_rows, atom_width = atom_feats.shape
    devices = lax.axis_size(BOTH)
    rows, cols = (lax.axis_size("row"), lax.axis_size("col"))
    row, col = (lax.axis_index("row"), lax.axis_index("col"))
    position = row * cols + col
    total_atoms = atom_rows * devices
    total_tokens = atom_counts.shape[0]
    first_atom = position * atom_rows
    blocks = atom_rows // QB
    offsets = key_starts - (
        QB * (position * blocks + jnp.arange(blocks, dtype=jnp.int32)) - KW // 2
    )
    offset_rows = (
        jnp.zeros((8, atom_width), jnp.bfloat16)
        .at[:blocks]
        .set(jnp.broadcast_to(offsets[:, None], (blocks, atom_width)).astype(jnp.bfloat16))
    )
    packed = jnp.concatenate([atom_feats, offset_rows], axis=0)
    prev1, next1 = (shifted(packed, 1), shifted(packed, -1))
    prev2, next2 = (shifted(atom_feats[32:], 2), shifted(atom_feats[:32], -2))
    token_ends = jnp.cumsum(atom_counts, dtype=jnp.int32)
    token_starts = token_ends - atom_counts
    edges = atom_rows * jnp.arange(devices + 1, dtype=jnp.int32)
    bases = jnp.sum((token_starts[None, :] < edges[:, None]).astype(jnp.int32), axis=1)
    base = lax.dynamic_index_in_dim(bases, position, 0, keepdims=False)
    pad = jnp.full((16,), total_atoms, jnp.int32)
    padded_starts = jnp.concatenate([jnp.zeros((1,), jnp.int32) - MOST, token_starts, pad])
    padded_ends = jnp.concatenate([jnp.zeros((1,), jnp.int32), token_ends, pad])
    low = lax.dynamic_slice_in_dim(padded_starts, base, 16, 0)[:, None]
    high = lax.dynamic_slice_in_dim(padded_ends, base, 16, 0)[:, None]
    ext = jnp.concatenate([prev2, prev1[:64], atom_feats, next1[:64], next2], axis=0)
    feats_q = jnp.concatenate([prev1[32:64], atom_feats, next1[:32]], axis=0)
    off4 = jnp.concatenate([prev1[65:66, :1], offset_rows[0:2, :1], next1[64:65, :1]], axis=0)
    starts4 = (
        off4.astype(jnp.int32)
        + first_atom
        - QB
        - KW // 2
        + QB * jnp.arange(4, dtype=jnp.int32)[:, None]
    )
    starts = jnp.repeat(starts4, QB, axis=0)
    atom_out, single = atom_part(
        ext,
        feats_q,
        starts,
        first_atom,
        total_atoms,
        (low, high),
        atom_gain,
        w_query,
        w_key,
        w_value,
        w_out,
        w_pool,
        w_back,
    )
    slots = atom_rows // FEWEST
    slot_single = single[1 : 1 + slots]
    slot_index = jnp.arange(slots, dtype=jnp.int32)[None, :]
    token_id = jnp.where(
        slot_index < (bases[1:] - bases[:-1])[:, None], bases[:-1, None] + slot_index, -1
    )
    row_slots = cols * slots
    row_single = lax.all_gather(slot_single, "col", axis=0, tiled=True)
    row_ids = lax.dynamic_slice_in_dim(token_id.reshape(rows, row_slots), row, 1, 0)
    lr = project(row_single, jnp.concatenate([w_left, w_right], axis=1))
    gathered = lax.all_gather(lr, "row", axis=0, tiled=True)
    opm = w_left.shape[1]
    row_tokens, col_tokens, pair_width = pair_state.shape
    all_ids = token_id.reshape(1, -1)
    want_left = row * row_tokens + jnp.arange(row_tokens, dtype=jnp.int32)[:, None]
    want_right = col * col_tokens + jnp.arange(col_tokens, dtype=jnp.int32)[:, None]
    left_rows = project((all_ids == want_left).astype(jnp.bfloat16), gathered[:, :opm])
    right_cols = project((all_ids == want_right).astype(jnp.bfloat16), gathered[:, opm:])
    own = total_tokens // devices
    place = jnp.arange(rows * own, dtype=jnp.int32)
    want_own = (place // own * cols + col) * own + place % own
    spread = project((row_ids == want_own[:, None]).astype(jnp.bfloat16), row_single)
    token_single = lax.psum_scatter(spread, "row", scatter_dimension=0, tiled=True)
    outer_table = jnp.einsum(
        "jb,abc->jac", right_cols, w_outer, preferred_element_type=jnp.float32
    ).astype(jnp.bfloat16)
    step_rows = math.gcd(row_tokens, 8)

    def pair_block(pieces):
        left_block, pair_piece = pieces
        outer_term = jnp.einsum(
            "ia,jac->ijc", left_block, outer_table, preferred_element_type=jnp.float32
        )
        summed = pair_piece.astype(jnp.float32) + outer_term
        normed_pair = layer_norm(summed, pair_gain).astype(jnp.bfloat16)
        gate_proj = jnp.einsum(
            "ijc,cf->ijf", normed_pair, w_gate, preferred_element_type=jnp.float32
        )
        lift_proj = jnp.einsum(
            "ijc,cf->ijf", normed_pair, w_lift, preferred_element_type=jnp.float32
        )
        hidden = (jax.nn.silu(gate_proj) * lift_proj).astype(jnp.bfloat16)
        return (
            summed + jnp.einsum("ijf,fc->ijc", hidden, w_drop, preferred_element_type=jnp.float32)
        ).astype(jnp.bfloat16)

    pair_out = lax.map(
        pair_block,
        (
            left_rows.reshape(-1, step_rows, left_rows.shape[1]),
            pair_state.reshape(-1, step_rows, col_tokens, pair_width),
        ),
    )
    return (atom_out, token_single, pair_out.reshape(row_tokens, col_tokens, pair_width))


def solution(mesh):
    whole = P(BOTH, None)
    in_specs = (whole, P(BOTH)) + (P(),) * 8 + (P("row", "col", None),) + (P(),) * 7
    out_specs = (whole, whole, P("row", "col", None))
    return jax.shard_map(
        per_device, mesh=mesh, in_specs=in_specs, out_specs=out_specs, check_vma=False
    )
```

profile of v0, /device:TPU:2, one launch (start us, length us, event | category | flops | bytes accessed | tf_op | source)
XLA Modules:
  0.0 333.0 jit_solution(10406786678176366872)
XLA Ops:
  7.2 0.7 subtract_convert_fusion
  8.0 0.8 pad_maximum_fusion
  8.8 1.9 collective-permute-start.1
  10.7 2.4 collective-permute-start
  13.1 0.7 fusion.95
  13.8 7.8 %collective-permute-start.3 = (bf16[32,128]{1,0:T(8,128)(2,1)S(1)}, bf16[32,128]{1,0:T(8,128)(2,1)S(1)}, u32[]{:S(2)}, u32[]{:S(2)}) collective-permute-start(bf16[32,128]{1,0:T(8,128)(2,1)S(1)} %get-tuple-element.133), channel_id=1, source_target_pairs={{2,0},{3,1},{4,2},{5,3},{6,4},{7,5},{8,6},{9,7},{10,8},{11,9},{12,... | collective-permute-start | bytes 24584 | tf_op jit(solution)/shard_map/ppermute | solution.py:19
  21.6 1.9 collective-permute-start.2
  23.6 1.0 reduce-window.9
  24.8 0.8 fusion.93
  25.6 0.6 convert_reduce_fusion
  26.3 0.6 dynamic_slice.21
  30.2 1.3 dynamic-slice.6
  32.1 0.5 slice.149
  32.7 0.5 slice.148
  33.2 1.4 fusion.89
  34.7 0.7 constant_dynamic-update-slice_fusion.1
  35.8 0.8 fusion.47
  36.6 1.0 convolution_convert_fusion.4
  37.6 1.0 convolution_convert_fusion.3
  41.5 21.2 %all_gather.6 = bf16[128,384]{1,0:T(8,128)(2,1)S(1)} all-gather(bf16[8,384]{1,0:T(8,128)(2,1)S(1)} %slice.169), channel_id=1, replica_groups=mesh['row'=32,'col'=16] {'col'}, dimensions={0}, use_global_device_ids=true | all-gather | bytes 104448 | tf_op jit(solution)/shard_map/all_gather | solution.py:177
  62.7 0.9 convolution_convert_fusion.1
  63.8 72.7 %all_gather.7 = bf16[4096,64]{0,1:T(8,128)(2,1)S(1)} all-gather(bf16[128,64]{0,1:T(8,128)(2,1)S(1)} %convolution_convert_fusion.5), channel_id=1, replica_groups=mesh['row'=32,'col'=16] {'row'}, dimensions={0}, use_global_device_ids=true | all-gather | bytes 540672 | tf_op jit(solution)/shard_map/all_gather | solution.py:180
  136.9 1.4 convolution_convert_fusion
  138.4 0.7 copy.59
  139.1 37.6 %while.11 = (s32[]{:T(128)}, bf16[8,8,128,128]{3,2,1,0:T(8,128)(2,1)}, bf16[8,8,128,128]{3,2,1,0:T(8,128)(2,1)}, bf16[8,8,32]{2,1,0:T(8,128)(2,1)S(1)}, bf16[128...) while((s32[]{:T(128)}, ...), condition=%wide.region_13.14_spmd, body=%wide.region_10.13_spmd.sunk | while | flops 415761408 | bytes 12229241 | solution.py:216
  139.1 1.0 constant_dynamic-slice_fusion.3
  141.3 0.4 fusion.132
  141.7 0.7 multiply_convert_fusion.5
  142.4 0.7 fusion.133
  143.1 0.7 copy_dynamic-update-slice_fusion.2
  143.9 1.0 constant_dynamic-slice_fusion.3
  146.0 0.4 fusion.132
  146.4 0.7 multiply_convert_fusion.5
  147.1 0.7 fusion.133
  147.8 0.7 copy_dynamic-update-slice_fusion.2
  148.5 1.0 constant_dynamic-slice_fusion.3
  151.0 0.7 multiply_convert_fusion.5
  151.8 0.7 fusion.133
  152.5 0.7 copy_dynamic-update-slice_fusion.2
  153.2 1.0 constant_dynamic-slice_fusion.3
  155.7 0.7 multiply_convert_fusion.5
  156.4 0.7 fusion.133
  157.2 0.7 copy_dynamic-update-slice_fusion.2
  157.9 1.0 constant_dynamic-slice_fusion.3
  160.0 0.4 fusion.132
  160.4 0.7 multiply_convert_fusion.5
  161.1 0.7 fusion.133
  161.9 0.7 copy_dynamic-update-slice_fusion.2
  162.6 1.0 constant_dynamic-slice_fusion.3
  165.1 0.7 multiply_convert_fusion.5
  165.8 0.7 fusion.133
  166.5 0.7 copy_dynamic-update-slice_fusion.2
  167.3 1.0 constant_dynamic-slice_fusion.3
  169.4 0.4 fusion.132
  169.8 0.7 multiply_convert_fusion.5
  170.5 0.7 fusion.133
  171.2 0.7 copy_dynamic-update-slice_fusion.2
  172.0 1.0 constant_dynamic-slice_fusion.3
  174.5 0.7 multiply_convert_fusion.5
  175.2 0.7 fusion.133
  175.9 0.7 copy_dynamic-update-slice_fusion.2
  176.7 0.9 fusion.24
  177.6 147.3 %all-reduce.4.cloned.1.call-done = bf16[128,384]{1,0:T(8,128)(2,1)} async-done(((bf16[128,384]{1,0:T(8,128)(2,1)}), bf16[128,384]{1,0:T(8,128)(2,1)}) %all-reduce.4.cloned.1.call-update) | async-done | bytes 98320
  324.9 1.3 constant_dynamic-slice_fusion.1
  (135 shorter events, 16.1 us)
Async XLA Ops:
  7.2 129.8 %copy-start = (bf16[32,32,128]{2,1,0:T(8,128)(2,1)S(1)}, bf16[32,32,128]{2,1,0:T(8,128)(2,1)}, u32[]{:S(2)}) copy-start(bf16[32,32,128]{2,1,0:T(8,128)(2,1)} %param.35) | copy-start | bytes 786436
  7.2 32.6 %copy-start.5 = (bf16[128,128]{1,0:T(8,128)(2,1)S(1)}, bf16[128,128]{1,0:T(8,128)(2,1)}, u32[]{:S(2)}) copy-start(bf16[128,128]{1,0:T(8,128)(2,1)} %param.28) | copy-start | bytes 98308
  7.2 317.7 %all-reduce.4.cloned.1.call-start = ((), (), s32[]{:S(2)}) async-start(), calls=%async_computation | async-start | bytes 196608
  8.8 23.4 %collective-permute-start.1 = (bf16[72,128]{1,0:T(8,128)(2,1)S(1)}, bf16[72,128]{1,0:T(8,128)(2,1)S(1)}, u32[]{:S(2)}, u32[]{:S(2)}) collective-permute-start(bf16[72,128]{1,0:T(8,128)(2,1)S(1)} %pad_maximum_fusion), channel_id=1, source_target_pairs={{1,0},{2,1},{3,2},{4,3},{5,4},{6,5},{7,6},{8,7},{9,8},{10,9},{11,1... | collective-permute-start | bytes 55304 | tf_op jit(solution)/shard_map/ppermute | solution.py:19
  10.7 22.0 %collective-permute-start = (bf16[72,128]{1,0:T(8,128)(2,1)S(1)}, bf16[72,128]{1,0:T(8,128)(2,1)S(1)}, u32[]{:S(2)}, u32[]{:S(2)}) collective-permute-start(bf16[72,128]{1,0:T(8,128)(2,1)S(1)} %pad_maximum_fusion), channel_id=1, source_target_pairs={{0,1},{1,2},{2,3},{3,4},{4,5},{5,6},{6,7},{7,8},{8,9},{9,10},{10,1... | collective-permute-start | bytes 55304 | tf_op jit(solution)/shard_map/ppermute | solution.py:19
  13.8 21.6 %collective-permute-start.3 = (bf16[32,128]{1,0:T(8,128)(2,1)S(1)}, bf16[32,128]{1,0:T(8,128)(2,1)S(1)}, u32[]{:S(2)}, u32[]{:S(2)}) collective-permute-start(bf16[32,128]{1,0:T(8,128)(2,1)S(1)} %get-tuple-element.133), channel_id=1, source_target_pairs={{2,0},{3,1},{4,2},{5,3},{6,4},{7,5},{8,6},{9,7},{10,8},{11,9},{12,... | collective-permute-start | bytes 24584 | tf_op jit(solution)/shard_map/ppermute | solution.py:19
  21.6 10.5 %collective-permute-start.2 = (bf16[32,128]{1,0:T(8,128)(2,1)S(1)}, bf16[32,128]{1,0:T(8,128)(2,1)S(1)}, u32[]{:S(2)}, u32[]{:S(2)}) collective-permute-start(bf16[32,128]{1,0:T(8,128)(2,1)S(1)} %get-tuple-element.134), channel_id=1, source_target_pairs={{0,2},{1,3},{2,4},{3,5},{4,6},{5,7},{6,8},{7,9},{8,10},{9,11},{10,... | collective-permute-start | bytes 24584 | tf_op jit(solution)/shard_map/ppermute | solution.py:19
  32.1 8.9 %copy-start.3 = (bf16[64,128]{1,0:T(8,128)(2,1)S(1)}, bf16[64,128]{1,0:T(8,128)(2,1)}, u32[]{:S(2)}) copy-start(bf16[64,128]{1,0:T(8,128)(2,1)} %param.22) | copy-start | bytes 49156
  32.1 8.9 %copy-start.11 = (bf16[128,128]{1,0:T(8,128)(2,1)S(1)}, bf16[128,128]{1,0:T(8,128)(2,1)}, u32[]{:S(2)}) copy-start(bf16[128,128]{1,0:T(8,128)(2,1)} %param.29) | copy-start | bytes 98308
  35.6 5.6 %copy-start.10 = (bf16[128,384]{1,0:T(8,128)(2,1)S(1)}, bf16[128,384]{1,0:T(8,128)(2,1)}, u32[]{:S(2)}) copy-start(bf16[128,384]{1,0:T(8,128)(2,1)} %param.30) | copy-start | bytes 294916
  38.9 24.7 %copy-start.6 = (bf16[384,32]{0,1:T(8,128)(2,1)S(1)}, bf16[384,32]{0,1:T(8,128)(2,1)}, u32[]{:S(2)}) copy-start(bf16[384,32]{0,1:T(8,128)(2,1)} %param.34) | copy-start | bytes 73732
  38.9 24.7 %copy-start.7 = (bf16[384,32]{0,1:T(8,128)(2,1)S(1)}, bf16[384,32]{0,1:T(8,128)(2,1)}, u32[]{:S(2)}) copy-start(bf16[384,32]{0,1:T(8,128)(2,1)} %param.33) | copy-start | bytes 73732
  136.4 2.6 copy-start.1
  136.4 2.6 copy-start.2
  136.4 2.6 copy-start.8
  136.4 2.7 copy-start.9
  139.1 37.6 %copy-start.4 = (bf16[384,128]{1,0:T(8,128)(2,1)S(1)}, bf16[384,128]{1,0:T(8,128)(2,1)}, u32[]{:S(2)}) copy-start(bf16[384,128]{1,0:T(8,128)(2,1)} %param.31) | copy-start | bytes 294916
Sparse Core Ops, SparseCore 0:
  63.7 261.1 all-reduce.3
where the time goes:
time: 334 us; the launch traced here: 333 us
  waiting for transfers between devices  147 us (44%)
  blocking collectives  93.9 us (28%)
  matrix products  26.1 us (8%)
  local copies, waits for them, and re-layouts  21.3 us (6%)
  between operations  17.1 us (5%)
  starting transfers between devices  14.1 us (4%)
  other arithmetic  12.9 us (4%)
    unnamed x2, waiting for transfers between devices  147 us
    all_gather x1, blocking collectives, per_device(): gathered = lax.all_gather(lr, 'row', axis=0, tiled=True)  72.7 us
    all_gather x1, blocking collectives, per_device(): row_single = lax.all_gather(slot_single, 'col', axis=0, tiled=True)  21.2 us
    ppermute x4, starting transfers between devices, shifted(): return lax.ppermute(block, BOTH, route)  14 us
    dynamic_slice x8, local copies, waits for them, and re-layouts, per_device(): lax.map(pair_block, (left_rows.reshape(-1, step_rows, left_rows.shape[1])...  7.78 us
  transfers between devices with their start and end apart: 5, of which 1 were waited for; matrix products, arithmetic and copies ran while one was open for 15% of the time, Pallas kernels for 0%

commit v1 on v0

--- a/solution.py
+++ b/solution.py
@@ -177,7 +177,9 @@
     row_single = lax.all_gather(slot_single, "col", axis=0, tiled=True)
     row_ids = lax.dynamic_slice_in_dim(token_id.reshape(rows, row_slots), row, 1, 0)
     lr = project(row_single, jnp.concatenate([w_left, w_right], axis=1))
-    gathered = lax.all_gather(lr, "row", axis=0, tiled=True)
+    gathered = jnp.concatenate(
+        lax.all_to_all(jnp.stack([lr] * lax.axis_size("row")), "row", 0, 0), axis=0
+    )
     opm = w_left.shape[1]
     row_tokens, col_tokens, pair_width = pair_state.shape
     all_ids = token_id.reshape(1, -1)

time: 334 us -> 388 us (1.16)
  waiting for transfers between devices: 147 us -> 253 us
  blocking collectives: 93.9 us -> 21.2 us
  starting transfers between devices: 14.1 us -> 34.1 us
    unnamed x2, waiting for transfers between devices: 147 us -> 253 us
    all_gather x1 -> x0, blocking collectives: 72.7 us -> none  [per_device(): gathered = lax.all_gather(lr, 'row', axis=0, tiled=True)]
    all_to_all x0 -> x1, starting transfers between devices: none -> 20 us  [per_device(): lax.all_to_all(jnp.stack([lr] * lax.axis_size('row')), 'row', 0, 0)]
  transfers between devices with their start and end apart: 5 -> 6, of which waited for: 1 -> 1; matrix products, arithmetic and copies ran while one was open for 15% -> 3% of each run, Pallas kernels for 0% -> 0%
where the time goes in v1:
time: 388 us; the launch traced here: 387 us
  waiting for transfers between devices  253 us (65%)
  starting transfers between devices  34.1 us (9%)
  matrix products  26.2 us (7%)
  local copies, waits for them, and re-layouts  22.2 us (6%)
  blocking collectives  21.2 us (5%)
  between operations  17.1 us (4%)
  other arithmetic  12.9 us (3%)
    unnamed x2, waiting for transfers between devices  253 us
    all_gather x1, blocking collectives, per_device(): row_single = lax.all_gather(slot_single, 'col', axis=0, tiled=True)  21.2 us
    all_to_all x1, starting transfers between devices, per_device(): lax.all_to_all(jnp.stack([lr] * lax.axis_size('row')), 'row', 0, 0)  20 us
    ppermute x4, starting transfers between devices, shifted(): return lax.ppermute(block, BOTH, route)  14 us
  transfers between devices with their start and end apart: 6, of which 1 were waited for; matrix products, arithmetic and copies ran while one was open for 3% of the time, Pallas kernels for 0%

profile of v1, /device:TPU:2, one launch (start us, length us, event | category | flops | bytes accessed | tf_op | source)
XLA Modules:
  0.0 387.3 jit_solution(17821790177145892687)
XLA Ops:
  7.2 0.7 subtract_convert_fusion
  8.0 0.8 pad_maximum_fusion
  8.8 1.9 collective-permute-start.1
  10.7 2.4 collective-permute-start
  13.1 0.7 fusion.95
  13.8 7.8 %collective-permute-start.3 = (bf16[32,128]{1,0:T(8,128)(2,1)S(1)}, bf16[32,128]{1,0:T(8,128)(2,1)S(1)}, u32[]{:S(2)}, u32[]{:S(2)}) collective-permute-start(bf16[32,128]{1,0:T(8,128)(2,1)S(1)} %get-tuple-element.142), channel_id=1, source_target_pairs={{2,0},{3,1},{4,2},{5,3},{6,4},{7,5},{8,6},{9,7},{10,8},{11,9},{12,... | collective-permute-start | bytes 24584 | tf_op jit(solution)/shard_map/ppermute | solution.py:19
  21.6 1.9 collective-permute-start.2
  23.6 1.0 reduce-window.9
  24.8 0.8 fusion.93
  25.6 0.6 convert_reduce_fusion
  26.2 0.6 dynamic_slice.21
  29.0 0.5 slice.149
  29.5 0.5 slice.148
  30.0 1.4 fusion.89
  31.6 0.7 constant_dynamic-update-slice_fusion.1
  32.6 0.8 fusion.47
  33.4 1.0 convolution_convert_fusion.4
  34.4 1.0 convolution_convert_fusion.3
  38.3 21.2 %all_gather.3 = bf16[128,384]{1,0:T(8,128)(2,1)S(1)} all-gather(bf16[8,384]{1,0:T(8,128)(2,1)S(1)} %slice.169), channel_id=1, replica_groups=mesh['row'=32,'col'=16] {'col'}, dimensions={0}, use_global_device_ids=true | all-gather | bytes 104448 | tf_op jit(solution)/shard_map/all_gather | solution.py:177
  59.7 0.9 stack.2
  60.6 20.0 %all-to-all-start = ((bf16[32,128,64]{1,2,0:T(8,128)(2,1)}), bf16[32,128,64]{1,2,0:T(8,128)(2,1)S(1)}, u32[]{:S(2)}, u32[]{:S(2)}) async-start(bf16[32,128,64]{1,2,0:T(8,128)(2,1)} %stack.2), calls=%async_computation | async-start | bytes 1048576 | tf_op jit(solution)/shard_map/all_to_all | solution.py:181
  81.6 1.3 dynamic-slice.6
  83.9 0.9 convolution_convert_fusion.1
  84.8 0.9 fusion.24
  85.6 253.1 %all-reduce.4.cloned.1.call-done = bf16[128,384]{1,0:T(8,128)(2,1)} async-done(((bf16[128,384]{1,0:T(8,128)(2,1)}), bf16[128,384]{1,0:T(8,128)(2,1)}) %all-reduce.4.cloned.1.call-update) | async-done | bytes 98320
  338.8 1.3 constant_dynamic-slice_fusion.1
  340.6 1.4 convolution_convert_fusion
  342.1 0.7 copy.73
  342.8 37.7 %while.11 = (s32[]{:T(128)}, bf16[8,8,128,128]{3,2,1,0:T(8,128)(2,1)}, bf16[8,8,128,128]{3,2,1,0:T(8,128)(2,1)}, bf16[8,8,32]{2,1,0:T(8,128)(2,1)S(1)}, bf16[128...) while((s32[]{:T(128)}, ...), condition=%wide.region_13.14_spmd, body=%wide.region_10.13_spmd.sunk | while | flops 415761408 | bytes 12229241 | solution.py:218
  342.8 1.0 constant_dynamic-slice_fusion.3
  345.3 0.7 multiply_convert_fusion.5
  346.1 0.7 fusion.134
  346.8 0.7 copy_dynamic-update-slice_fusion.2
  347.5 1.0 constant_dynamic-slice_fusion.3
  349.6 0.4 fusion.133
  350.1 0.7 multiply_convert_fusion.5
  350.8 0.7 fusion.134
  351.5 0.7 copy_dynamic-update-slice_fusion.2
  352.3 1.0 constant_dynamic-slice_fusion.3
  354.3 0.4 fusion.133
  354.8 0.7 multiply_convert_fusion.5
  355.5 0.7 fusion.134
  356.2 0.7 copy_dynamic-update-slice_fusion.2
  357.0 1.0 constant_dynamic-slice_fusion.3
  359.5 0.7 multiply_convert_fusion.5
  360.2 0.7 fusion.134
  360.9 0.7 copy_dynamic-update-slice_fusion.2
  361.7 1.0 constant_dynamic-slice_fusion.3
  364.2 0.7 multiply_convert_fusion.5
  364.9 0.7 fusion.134
  365.6 0.7 copy_dynamic-update-slice_fusion.2
  366.4 1.0 constant_dynamic-slice_fusion.3
  368.9 0.7 multiply_convert_fusion.5
  369.6 0.7 fusion.134
  370.3 0.7 copy_dynamic-update-slice_fusion.2
  371.1 1.0 constant_dynamic-slice_fusion.3
  373.2 0.4 fusion.133
  373.6 0.7 multiply_convert_fusion.5
  374.3 0.7 fusion.134
  375.0 0.7 copy_dynamic-update-slice_fusion.2
  375.8 1.0 constant_dynamic-slice_fusion.3
  378.3 0.7 multiply_convert_fusion.5
  379.0 0.7 fusion.134
  379.7 0.7 copy_dynamic-update-slice_fusion.2
  (138 shorter events, 16.6 us)
Async XLA Ops:
  7.2 333.5 %copy-start = (bf16[32,32,128]{2,1,0:T(8,128)(2,1)S(1)}, bf16[32,32,128]{2,1,0:T(8,128)(2,1)}, u32[]{:S(2)}) copy-start(bf16[32,32,128]{2,1,0:T(8,128)(2,1)} %param.35) | copy-start | bytes 786436
  7.2 29.4 %copy-start.5 = (bf16[128,128]{1,0:T(8,128)(2,1)S(1)}, bf16[128,128]{1,0:T(8,128)(2,1)}, u32[]{:S(2)}) copy-start(bf16[128,128]{1,0:T(8,128)(2,1)} %param.28) | copy-start | bytes 98308
  8.8 20.2 %collective-permute-start.1 = (bf16[72,128]{1,0:T(8,128)(2,1)S(1)}, bf16[72,128]{1,0:T(8,128)(2,1)S(1)}, u32[]{:S(2)}, u32[]{:S(2)}) collective-permute-start(bf16[72,128]{1,0:T(8,128)(2,1)S(1)} %pad_maximum_fusion), channel_id=1, source_target_pairs={{1,0},{2,1},{3,2},{4,3},{5,4},{6,5},{7,6},{8,7},{9,8},{10,9},{11,1... | collective-permute-start | bytes 55304 | tf_op jit(solution)/shard_map/ppermute | solution.py:19
  10.7 18.8 %collective-permute-start = (bf16[72,128]{1,0:T(8,128)(2,1)S(1)}, bf16[72,128]{1,0:T(8,128)(2,1)S(1)}, u32[]{:S(2)}, u32[]{:S(2)}) collective-permute-start(bf16[72,128]{1,0:T(8,128)(2,1)S(1)} %pad_maximum_fusion), channel_id=1, source_target_pairs={{0,1},{1,2},{2,3},{3,4},{4,5},{5,6},{6,7},{7,8},{8,9},{9,10},{10,1... | collective-permute-start | bytes 55304 | tf_op jit(solution)/shard_map/ppermute | solution.py:19
  13.8 18.5 %collective-permute-start.3 = (bf16[32,128]{1,0:T(8,128)(2,1)S(1)}, bf16[32,128]{1,0:T(8,128)(2,1)S(1)}, u32[]{:S(2)}, u32[]{:S(2)}) collective-permute-start(bf16[32,128]{1,0:T(8,128)(2,1)S(1)} %get-tuple-element.142), channel_id=1, source_target_pairs={{2,0},{3,1},{4,2},{5,3},{6,4},{7,5},{8,6},{9,7},{10,8},{11,9},{12,... | collective-permute-start | bytes 24584 | tf_op jit(solution)/shard_map/ppermute | solution.py:19
  21.6 7.3 %collective-permute-start.2 = (bf16[32,128]{1,0:T(8,128)(2,1)S(1)}, bf16[32,128]{1,0:T(8,128)(2,1)S(1)}, u32[]{:S(2)}, u32[]{:S(2)}) collective-permute-start(bf16[32,128]{1,0:T(8,128)(2,1)S(1)} %get-tuple-element.143), channel_id=1, source_target_pairs={{0,2},{1,3},{2,4},{3,5},{4,6},{5,7},{6,8},{7,9},{8,10},{9,11},{10,... | collective-permute-start | bytes 24584 | tf_op jit(solution)/shard_map/ppermute | solution.py:19
  28.9 8.9 %copy-start.3 = (bf16[64,128]{1,0:T(8,128)(2,1)S(1)}, bf16[64,128]{1,0:T(8,128)(2,1)}, u32[]{:S(2)}) copy-start(bf16[64,128]{1,0:T(8,128)(2,1)} %param.22) | copy-start | bytes 49156
  28.9 8.9 %copy-start.11 = (bf16[128,128]{1,0:T(8,128)(2,1)S(1)}, bf16[128,128]{1,0:T(8,128)(2,1)}, u32[]{:S(2)}) copy-start(bf16[128,128]{1,0:T(8,128)(2,1)} %param.29) | copy-start | bytes 98308
  32.4 5.6 %copy-start.10 = (bf16[128,384]{1,0:T(8,128)(2,1)S(1)}, bf16[128,384]{1,0:T(8,128)(2,1)}, u32[]{:S(2)}) copy-start(bf16[128,384]{1,0:T(8,128)(2,1)} %param.30) | copy-start | bytes 294916
  35.4 24.2 %copy-start.6 = (bf16[384,32]{0,1:T(8,128)(2,1)S(1)}, bf16[384,32]{0,1:T(8,128)(2,1)}, u32[]{:S(2)}) copy-start(bf16[384,32]{0,1:T(8,128)(2,1)} %param.34) | copy-start | bytes 73732
  35.4 24.1 %copy-start.7 = (bf16[384,32]{0,1:T(8,128)(2,1)S(1)}, bf16[384,32]{0,1:T(8,128)(2,1)}, u32[]{:S(2)}) copy-start(bf16[384,32]{0,1:T(8,128)(2,1)} %param.33) | copy-start | bytes 73732
  37.6 47.2 %copy-start.4 = (bf16[384,128]{1,0:T(8,128)(2,1)S(1)}, bf16[384,128]{1,0:T(8,128)(2,1)}, u32[]{:S(2)}) copy-start(bf16[384,128]{1,0:T(8,128)(2,1)} %param.31) | copy-start | bytes 294916
  60.6 279.4 %all-to-all-start = ((bf16[32,128,64]{1,2,0:T(8,128)(2,1)}), bf16[32,128,64]{1,2,0:T(8,128)(2,1)S(1)}, u32[]{:S(2)}, u32[]{:S(2)}) async-start(bf16[32,128,64]{1,2,0:T(8,128)(2,1)} %stack.2), calls=%async_computation | async-start | bytes 1048576 | tf_op jit(solution)/shard_map/all_to_all | solution.py:181
  80.7 258.1 %all-reduce.4.cloned.1.call-start = ((), (), s32[]{:S(2)}) async-start(), calls=%async_computation.1 | async-start | bytes 196608
  340.1 2.7 copy-start.1
  340.1 2.7 copy-start.2
  340.1 2.7 copy-start.8
  340.2 2.7 copy-start.9
Sparse Core Ops, SparseCore 0:
  84.9 253.8 all-reduce.3
